TPU v7x, 512 devices: a whole 4x8x8 slice. The times are simulated.
512 devices in a mesh: row: 32 (over z, x), rep: 8 (over y), feat: 2 (over core).
Axes of the slice: x: 4, y: 8, z: 8, core: 2. Of those that a mesh axis runs over, the one named last changes fastest.
Arguments:
- features: bfloat16 [32768, 256], P(('row', 'rep'), 'feat'), may hold values from -6 to 6
- weight: float32 [256, 256], replicated, may hold values from -0.375 to 0.375
- layer_bias: float32 [256], replicated, may hold values from -3 to 3
- cotangent: float32 [32768, 256], P(('row', 'rep'), 'feat'), may hold values from -6 to 6
- adj_tiles: bfloat16 [32, 8, 8, 8, 128, 128], P('row', 'rep', None, 'feat'), may hold values from -0.3125 to 0.3125
- tile_source: int32 [32, 8, 8, 8], P('row', 'rep', None, 'feat'), may hold values from 0 to 31
- tile_count: int32 [32, 8, 8], P('row', 'rep'), may hold values from 1 to 8, as said below
Outputs:
- output: float32 [32768, 256], P(('row', 'rep'), 'feat')
- grad_features: float32 [32768, 256], P(('row', 'rep'), 'feat')
- grad_weight: float32 [256, 256], P(None, 'feat')
- grad_bias: float32 [256], P('feat')
Inputs may be any that keep to these rules, and one draw needn't show every extreme that they name: `tile_count`: each list has at least one live slot; some list in every draw has all 8 slots live.
All inputs are finite; a program needn't handle non-finite values.
Results may differ from a plain program's by a relative error of at most 0.0029.
Values may be sent and summed in bfloat16 or wider, within the bound.
No kernel may reach another device: no remote copies, remote signals or barrier semaphores. Data moves between devices by JAX's collectives and lax.ppermute only.
A program may use at most 64 MiB of HBM per device.

v0:
```python
import jax
import jax.numpy as jnp
from jax import lax
from jax.sharding import PartitionSpec as P


def local(features, weight, layer_bias, cotangent, adj_tiles, tile_source, tile_count):
    highest = lax.Precision.HIGHEST
    block_rows = features.shape[0]
    half_width = features.shape[1]
    feat_count = lax.axis_size("feat")
    width = half_width * feat_count
    own_feat = lax.axis_index("feat")
    own_rep = lax.axis_index("rep")
    local_tiles = adj_tiles[0, 0]
    sources = tile_source[0, 0]
    counts = tile_count[0, 0]
    dest_count, slots_half = sources.shape
    slot_ids = own_feat * slots_half + jnp.arange(slots_half, dtype=jnp.int32)
    live_mask = slot_ids[None, :] < counts[:, None]
    masked = jnp.where(live_mask[:, :, None, None], local_tiles, jnp.zeros_like(local_tiles))
    pieces = lax.all_gather(features[None], ("row", "feat"), axis=0, tiled=True)
    piece_groups = pieces.shape[0] // feat_count
    source_panel = (
        pieces.reshape(piece_groups, feat_count, block_rows, half_width)
        .transpose(0, 2, 1, 3)
        .reshape(piece_groups, block_rows, width)
    )
    group_count = source_panel.shape[0]
    chosen = jnp.take(source_panel, sources, axis=0)
    partial_value = jnp.einsum("dkij,dkjc->dic", masked, chosen, preferred_element_type=jnp.float32)
    group_aggregate = lax.psum(partial_value, ("rep", "feat"))
    own_aggregate = lax.dynamic_index_in_dim(group_aggregate, own_rep, 0, keepdims=False)
    weight_cols = lax.dynamic_slice_in_dim(weight, own_feat * half_width, half_width, 1)
    bias_cols = lax.dynamic_slice_in_dim(layer_bias, own_feat * half_width, half_width, 0)
    preact_cols = jnp.dot(own_aggregate, weight_cols, precision=highest) + bias_cols
    sigmoid_val = jax.nn.sigmoid(preact_cols)
    output = preact_cols * sigmoid_val
    slope_cols = cotangent * (sigmoid_val * (1.0 + preact_cols * (1.0 - sigmoid_val)))
    grad_part = jnp.dot(slope_cols, weight_cols.T, precision=highest)
    gathered = lax.all_gather(grad_part[None], ("rep", "feat"), axis=0, tiled=True)
    grad_aggregate = jnp.sum(
        gathered.reshape(dest_count, feat_count, block_rows, width), axis=1
    ).astype(jnp.bfloat16)
    weight_term = jnp.dot(own_aggregate.T, slope_cols, precision=highest)
    bias_term = jnp.sum(slope_cols, axis=0)
    grad_weight, grad_bias = lax.psum((weight_term, bias_term), ("row", "rep"))

    def add_dest(accumulated, dest_items):
        tile_list, source_list, grad_rows = dest_items
        contrib = jnp.einsum(
            "kij,ic->kjc", tile_list, grad_rows, preferred_element_type=jnp.float32
        )
        return (accumulated.at[source_list].add(contrib), None)

    start_total = jnp.zeros((group_count, block_rows, width), jnp.float32)
    summed, unused = lax.scan(add_dest, start_total, (masked, sources, grad_aggregate))
    terms_all = (
        summed.reshape(group_count, block_rows, feat_count, half_width)
        .transpose(0, 2, 1, 3)
        .reshape(group_count * feat_count * block_rows, half_width)
    )
    grad_features = lax.psum_scatter(terms_all, ("row", "feat"), scatter_dimension=0, tiled=True)
    return (output, grad_features, grad_weight, grad_bias)


def solution(mesh):
    in_specs = (
        P(("row", "rep"), "feat"),
        P(),
        P(),
        P(("row", "rep"), "feat"),
        P("row", "rep", None, "feat", None, None),
        P("row", "rep", None, "feat"),
        P("row", "rep", None),
    )
    out_specs = (P(("row", "rep"), "feat"), P(("row", "rep"), "feat"), P(None, "feat"), P("feat"))
    return jax.shard_map(local, mesh=mesh, in_specs=in_specs, out_specs=out_specs, check_vma=False)
```

profile of v0, /device:TPU:0, one launch (start us, length us, event | category | flops | bytes accessed | tf_op | source)
XLA Modules:
  0.0 995.5 jit_solution(4761539337155817513)
XLA Ops:
  7.2 0.7 all-gather.5.cloned.1.call-update
  8.0 0.7 compare_and_fusion
  8.8 0.7 compare_select_fusion.1
  9.6 1.6 copy.24
  11.5 82.8 %all-gather.5.cloned.1.call-done = bf16[8192,128]{1,0:T(8,128)(2,1)} async-done(((bf16[128,128]{1,0:T(8,128)(2,1)}), bf16[8192,128]{1,0:T(8,128)(2,1)}) %all-gather.5.cloned.1.call-update) | async-done | bytes 2097168 | tf_op jit(solution)/shard_map/all_gather | solution.py:22
  94.4 3.2 copy.26
  97.6 2.2 gather_fusion
  99.7 2.9 copy.28
  102.6 1.6 fusion.11
  104.4 114.9 %all-reduce.3.cloned.1.call-done = f32[8,128,256]{2,1,0:T(8,128)} async-done(((f32[8,128,256]{2,1,0:T(8,128)}), f32[8,128,256]{2,1,0:T(8,128)}) %all-reduce.3.cloned.1.call-update) | async-done | bytes 1048592 | tf_op jit(solution)/shard_map/psum | solution.py:32
  219.3 1.8 fusion.28
  221.1 0.9 fusion.18
  222.2 2.0 fusion.15
  224.3 40.1 %all-gather.7.cloned.1.call-done = f32[2048,256]{1,0:T(8,128)} async-done(((f32[128,256]{1,0:T(8,128)}), f32[2048,256]{1,0:T(8,128)}) %all-gather.7.cloned.1.call-update) | async-done | bytes 2097168 | tf_op jit(solution)/shard_map/all_gather | solution.py:41
  264.3 1.8 reduce_sum.18
  266.1 2.5 broadcast_in_dim.39
  268.6 23.0 %while.10 = (s32[]{:T(128)}, f32[32,128,256]{2,1,0:T(8,128)}, s32[8,4]{1,0:T(8,128)S(1)}, bf16[8,4,128,128]{2,3,1,0:T(8,128)(2,1)S(1)}, bf16[8,128,256]{2,1,0:T(8,128)(2,1)S(1)}, /*index=5*/s32[]{:T(128)}) while((s32[]{:T(128)}, f32[32,128,256]{2,1,0:T(8,128)}, s32[8,4]{1,0:T(8,128)S(1)}, bf16[8,4,128,128]{2,3,1,0:T(8,128)(2,1)S(1)}, ...), condition=%wide.region_4.5_spmd, body=%wide.region_2.4_spmd.sunk | while | flops 33685516 | bytes 2294913 | solution.py:57
  268.6 0.2 fusion.40
  268.8 2.7 scatter_fusion
  271.7 2.7 scatter_fusion
  274.4 0.2 fusion.40
  274.6 2.7 scatter_fusion
  277.5 2.7 scatter_fusion
  280.1 0.2 fusion.40
  280.3 2.7 scatter_fusion
  283.3 2.6 scatter_fusion
  285.9 0.2 fusion.40
  286.1 2.7 scatter_fusion
  289.0 2.7 scatter_fusion
  291.6 4.7 copy_bitcast_fusion
  296.4 691.0 %psum.23 = f32[128]{0:T(128)} all-reduce(f32[128]{0:T(128)S(1)} %get-tuple-element.57), channel_id=1, replica_groups=mesh['row'=32,'rep'=8,'feat'=2] {'row','rep'}, use_global_device_ids=true, to_apply=%region_8.9 | all-reduce | flops 128 | bytes 1024 | tf_op jit(solution)/shard_map/psum | solution.py:47
  987.4 1.6 copy.47
  (42 shorter events, 1.8 us)
Async XLA Ops:
  7.2 212.2 %copy-start = (f32[256,256]{1,0:T(8,128)S(1)}, f32[256,256]{1,0:T(8,128)}, u32[]{:S(2)}) copy-start(f32[256,256]{1,0:T(8,128)} %param.10) | copy-start | bytes 786436
  7.2 4.1 copy-start.2
  7.2 87.2 %all-gather.5.cloned.1.call-start = ((), (), s32[]{:S(2)}) async-start(), calls=%async_computation.4 | async-start | bytes 2129920 | tf_op jit(solution)/shard_map/all_gather | solution.py:22
  7.9 211.4 %all-reduce.3.cloned.1.call-start = ((), (), s32[]{:S(2)}) async-start(), calls=%async_computation.1 | async-start | bytes 2097152 | tf_op jit(solution)/shard_map/psum | solution.py:32
  102.6 1.7 copy-start.4
  102.6 116.7 %copy-start.3 = (f32[128,128]{1,0:T(8,128)S(1)}, f32[128,128]{1,0:T(8,128)}, u32[]{:S(2)}) copy-start(f32[128,128]{1,0:T(8,128)} %param.12) | copy-start | bytes 196612
  102.6 119.5 %copy-start.1 = (s32[1,1,8,4]{2,3,1,0:T(4,128)S(1)}, s32[1,1,8,4]{2,3,1,0:T(4,128)}, u32[]{:S(2)}) copy-start(s32[1,1,8,4]{2,3,1,0:T(4,128)} %param.14) | copy-start | bytes 388
  104.2 160.1 %all-gather.7.cloned.1.call-start = ((), (), s32[]{:S(2)}) async-start(), calls=%async_computation.5 | async-start | bytes 2228224 | tf_op jit(solution)/shard_map/all_gather | solution.py:41
  222.1 765.3 %all-reduce.5.cloned.1.call-start = ((), (), s32[]{:S(2)}) async-start(), calls=%async_computation.3 | async-start | bytes 262144 | tf_op jit(solution)/shard_map/psum | solution.py:47
  224.2 763.2 %reduce-scatter.2.cloned.1.call-start = ((), (), s32[]{:S(2)}) async-start(), calls=%async_computation.2 | async-start | bytes 4259840 | tf_op jit(solution)/shard_map/reduce_scatter | solution.py:63
Sparse Core Ops, SparseCore 0:
  11.3 82.9 all-gather.4
  104.4 114.8 all-reduce.2
  222.2 42.0 all-gather.6
  269.1 231.4 all-reduce.4
  505.8 149.6 reduce-scatter.1
where the time goes:
time: 996 us
  blocking collectives  691 us (69%)
  waiting for transfers between devices  239 us (24%)
  other arithmetic  24.8 us (2%)
  local copies, waits for them, and re-layouts  19.1 us (2%)
  between operations  13.9 us (1%)
    psum x1, blocking collectives, local(): grad_weight, grad_bias = lax.psum((weight_term, bias_term), ('row', 'rep'))  691 us
    psum x1, waiting for transfers between devices, local(): group_aggregate = lax.psum(partial_value, ('rep', 'feat'))  115 us
    all_gather x1, waiting for transfers between devices, local(): pieces = lax.all_gather(features[None], ('row', 'feat'), axis=0, tiled=True)  82.8 us
    all_gather x1, waiting for transfers between devices, local(): lax.all_gather(grad_part[None], ('rep', 'feat'), axis=0, tiled=True)  40.1 us
    scatter-add x8, other arithmetic, add_dest(): return (accumulated.at[source_list].add(contrib), None)  21.3 us
  transfers between devices with their start and end apart: 5, of which 3 were waited for; matrix products, arithmetic and copies ran while one was open for 4% of the time, Pallas kernels for 0%

commit v1 on v0

v1 whole, which is shorter than its diff:
```python
import jax
import jax.numpy as jnp
from jax import lax
from jax.experimental import pallas as pl
from jax.experimental.pallas import tpu as pltpu
from jax.sharding import PartitionSpec as P

BF = jnp.bfloat16
F32 = jnp.float32
HI = lax.Precision.HIGHEST
VM = pl.BlockSpec(memory_space=pltpu.VMEM)
SM = pl.BlockSpec(memory_space=pltpu.SMEM)


def slot_lists(own_ref, peer_ref, feat):
    return ((own_ref, feat), (peer_ref, 1 - feat))


def forward_kernel(count_ref, source_ref, own_ref, peer_ref, panel_ref, out_ref):
    feat = lax.axis_index("feat")
    dests, half = own_ref.shape[:2]
    for d in range(dests):
        lefts, rights = [], []
        for tiles_ref, side in slot_lists(own_ref, peer_ref, feat):
            for j in range(half):
                block = panel_ref[source_ref[side, d, j]]
                live = side * half + j < count_ref[d]
                lefts.append(tiles_ref[d, j])
                rights.append(jnp.where(live, block, jnp.zeros_like(block)))
        out_ref[d] = jnp.dot(
            jnp.concatenate(lefts, axis=1),
            jnp.concatenate(rights, axis=0),
            preferred_element_type=F32,
        )


def collect_kernel(parts_ref, cotangent_ref, out_ref):
    rows = cotangent_ref.shape[0]
    total = parts_ref[0]
    for p in range(1, parts_ref.shape[0]):
        total = total + parts_ref[p]
    out_ref[:rows] = total
    out_ref[rows:] = cotangent_ref[...]


def node_kernel(both_ref, weight_ref, bias_ref, out_ref, pay_ref):
    first = lax.axis_index("feat") == 0
    rows, cols = out_ref.shape
    reps = pay_ref.shape[0]
    aggregate = jnp.concatenate([both_ref[:rows], both_ref[2 * rows : 3 * rows]], axis=1)
    cotangent = jnp.concatenate([both_ref[rows : 2 * rows], both_ref[3 * rows :]], axis=1)
    preact = jnp.dot(aggregate, weight_ref[...], precision=HI, preferred_element_type=F32) + bias_ref[...]
    sig = jax.nn.sigmoid(preact)
    output = preact * sig
    slope = cotangent * (sig * (1.0 + preact * (1.0 - sig)))
    out_ref[...] = jnp.where(first, output[:, :cols], output[:, cols:])
    slope_own = jnp.where(first, slope[:, :cols], slope[:, cols:])
    weight_rows = jnp.where(first, weight_ref[:cols], weight_ref[cols:])
    grad_t = lax.dot_general(
        weight_rows, slope, (((1,), (1,)), ((), ())), precision=HI, preferred_element_type=F32
    ).astype(BF)
    weight_term = lax.dot_general(
        aggregate, slope_own, (((0,), (0,)), ((), ())), precision=HI, preferred_element_type=F32
    )
    bias_term = jnp.sum(slope_own, axis=0, keepdims=True)
    chunk = weight_term.shape[0] // reps
    pad = jnp.where(lax.broadcasted_iota(jnp.int32, (8, cols), 0) == 0, bias_term, 0.0)
    for q in range(reps):
        piece = jnp.concatenate([weight_term[q * chunk : (q + 1) * chunk], pad], axis=0)
        upper = piece.astype(BF)
        lower = (piece - upper.astype(F32)).astype(BF)
        pay_ref[q, :rows] = grad_t
        pay_ref[q, rows : rows + chunk + 8] = upper
        pay_ref[q, rows + chunk + 8 :] = lower


def backward_kernel(count_ref, source_ref, own_ref, peer_ref, pay_ref, out_ref, total_ref, terms_ref):
    feat = lax.axis_index("feat")
    dests, half, rows = own_ref.shape[:3]
    extra = out_ref.shape[1] - rows
    total_ref[...] = jnp.zeros_like(total_ref)
    for d in range(dests):
        grad_t = pay_ref[d, :rows]
        for h, (tiles_ref, side) in enumerate(slot_lists(own_ref, peer_ref, feat)):
            product = jnp.dot(
                grad_t,
                jnp.concatenate([tiles_ref[d, j] for j in range(half)], axis=1),
                preferred_element_type=F32,
            )
            for j in range(half):
                terms_ref[(d * 2 + h) * half + j] = product[:, j * rows : (j + 1) * rows]
    for d in range(dests):
        for h, (tiles_ref, side) in enumerate(slot_lists(own_ref, peer_ref, feat)):
            for j in range(half):

                @pl.when(side * half + j < count_ref[d])
                def _(d=d, h=h, j=j, side=side):
                    source = source_ref[side, d, j]
                    total_ref[source] = total_ref[source] + terms_ref[(d * 2 + h) * half + j]

    piece = jnp.zeros((extra, rows), F32)
    for q in range(pay_ref.shape[0]):
        piece = piece + pay_ref[q, rows : rows + extra].astype(F32) + pay_ref[q, rows + extra :].astype(F32)
    piece = piece.astype(BF)
    for s in range(out_ref.shape[0]):
        out_ref[s, :rows] = total_ref[s].astype(BF)
        out_ref[s, rows:] = piece


def finish_kernel(parts_ref, grad_ref, piece_ref):
    rows = grad_ref.shape[0]
    total = parts_ref[0].astype(F32)
    for s in range(1, parts_ref.shape[0]):
        total = total + parts_ref[s].astype(F32)
    grad_ref[...] = total[:rows].T
    for q in range(piece_ref.shape[0]):
        piece_ref[q] = total[rows:]


def shape(dims, dtype):
    return jax.ShapeDtypeStruct(dims, dtype)


def local(features, weight, layer_bias, cotangent, adj_tiles, tile_source, tile_count):
    rows, cols = features.shape
    n_row = lax.axis_size("row")
    own = adj_tiles[0, 0]
    counts = tile_count[0, 0]
    dests, half = own.shape[:2]
    reps = lax.axis_size("rep")
    width = weight.shape[0]
    extra = width // reps + 8
    peer = lax.ppermute(own, "feat", [(0, 1), (1, 0)])
    sources = lax.all_gather(tile_source[0, 0], "feat")
    panel = lax.all_to_all(jnp.broadcast_to(features[None], (n_row, rows, cols)), "row", 0, 0, tiled=True)
    partial = pl.pallas_call(
        forward_kernel,
        out_shape=shape((dests, rows, cols), F32),
        in_specs=[SM, SM, VM, VM, VM],
        out_specs=VM,
    )(counts, sources, own, peer, panel)
    parts = lax.all_to_all(partial, "rep", 0, 0, tiled=True)
    stacked = pl.pallas_call(
        collect_kernel, out_shape=shape((2 * rows, cols), F32), in_specs=[VM, VM], out_specs=VM
    )(parts, cotangent)
    both = lax.all_gather(stacked, "feat", axis=0, tiled=True)
    output, pay = pl.pallas_call(
        node_kernel,
        out_shape=(shape((rows, cols), F32), shape((reps, rows + 2 * extra, cols), BF)),
        in_specs=[VM, VM, VM],
        out_specs=(VM, VM),
    )(both, weight, layer_bias[None])
    pay = lax.all_to_all(pay, "rep", 0, 0, tiled=True)
    sends = pl.pallas_call(
        backward_kernel,
        out_shape=shape((n_row, rows + extra, cols), BF),
        in_specs=[SM, SM, VM, VM, VM],
        out_specs=VM,
        scratch_shapes=[
            pltpu.VMEM((n_row, cols, rows), F32),
            pltpu.VMEM((dests * 2 * half, cols, rows), F32),
        ],
    )(counts, sources, own, peer, pay)
    arrived = lax.all_to_all(sends, "row", 0, 0, tiled=True)
    grad_features, pieces = pl.pallas_call(
        finish_kernel,
        out_shape=(shape((rows, cols), F32), shape((reps, extra, cols), F32)),
        in_specs=[VM],
        out_specs=(VM, VM),
    )(arrived)
    pieces = lax.all_to_all(pieces, "rep", 0, 0, tiled=True)
    grad_weight = pieces[:, : extra - 8].reshape(width, cols)
    grad_bias = pieces[0, extra - 8]
    return output, grad_features, grad_weight, grad_bias


def solution(mesh):
    in_specs = (
        P(("row", "rep"), "feat"),
        P(),
        P(),
        P(("row", "rep"), "feat"),
        P("row", "rep", None, "feat", None, None),
        P("row", "rep", None, "feat"),
        P("row", "rep", None),
    )
    out_specs = (P(("row", "rep"), "feat"), P(("row", "rep"), "feat"), P(None, "feat"), P("feat"))
    return jax.shard_map(local, mesh=mesh, in_specs=in_specs, out_specs=out_specs, check_vma=False)
```

time: 996 us -> 163 us (0.16)
  the two profiles are of different devices: /device:TPU:0 before, /device:TPU:8 now
where the time goes in v1:
time: 163 us; the launch traced here: 162 us
  blocking collectives  104 us (64%)
  waiting for transfers between devices  22.8 us (14%)
  starting transfers between devices  15.1 us (9%)
  Pallas kernels  14.2 us (9%)
  local copies, waits for them, and re-layouts  4.88 us (3%)
    all_to_all x1, blocking collectives, local(): arrived = lax.all_to_all(sends, 'row', 0, 0, tiled=True)  42.2 us
    all_to_all x1, waiting for transfers between devices, local(): lax.all_to_all(jnp.broadcast_to(features[None], (n_row, rows, cols)), 'ro...  22.8 us
    all_to_all x1, blocking collectives, local(): parts = lax.all_to_all(partial, 'rep', 0, 0, tiled=True)  21.6 us
    all_to_all x1, blocking collectives, local(): pay = lax.all_to_all(pay, 'rep', 0, 0, tiled=True)  20.3 us
    all_to_all x1, blocking collectives, local(): pieces = lax.all_to_all(pieces, 'rep', 0, 0, tiled=True)  14.2 us
    all_to_all x1, starting transfers between devices, local(): lax.all_to_all(jnp.broadcast_to(features[None], (n_row, rows, cols)), 'ro...  13.2 us
    pallas_call x1, Pallas kernels, local(): pl.pallas_call(backward_kernel, out_shape=shape((n_row, rows + extra, col...  4.38 us
    all_gather x1, blocking collectives, local(): both = lax.all_gather(stacked, 'feat', axis=0, tiled=True)  3.52 us
  transfers between devices with their start and end apart: 2, of which 1 were waited for; matrix products, arithmetic and copies ran while one was open for 0% of the time, Pallas kernels for 0%

profile of v1, /device:TPU:8, one launch (start us, length us, event | category | flops | bytes accessed | tf_op | source)
XLA Modules:
  0.0 162.0 jit_solution(4894046835632330888)
XLA Ops:
  0.6 0.0 copy-start.1
  0.6 0.0 copy-start.3
  0.7 2.0 %broadcast_in_dim.4 = bf16[32,128,128]{2,1,0:T(8,128)(2,1)} broadcast(bf16[128,128]{1,0:T(8,128)(2,1)} %param.7), dimensions={1,2} | broadcast | bytes 1081344 | tf_op jit(solution)/shard_map/broadcast_in_dim | solution.py:135
  2.7 13.2 %all-to-all-start = ((bf16[32,128,128]{2,1,0:T(8,128)(2,1)}), bf16[32,128,128]{2,1,0:T(8,128)(2,1)S(1)}, u32[]{:S(2)}, u32[]{:S(2)}) async-start(bf16[32,128,128]{2,1,0:T(8,128)(2,1)} %broadcast_in_dim.4), calls=%async_computation | async-start | bytes 2097152 | tf_op jit(solution)/shard_map/all_to_all | solution.py:135
  15.9 0.0 copy-done.1
  15.9 1.9 %collective-permute-start = (bf16[8,4,128,128]{3,2,1,0:T(8,128)(2,1)S(1)}, bf16[8,4,128,128]{3,2,1,0:T(8,128)(2,1)S(1)}, u32[]{:S(2)}, u32[]{:S(2)}) collective-permute-start(bf16[8,4,128,128]{3,2,1,0:T(8,128)(2,1)S(1)} %bitcast.9), channel_id=1, source_target_pairs={{0,1},{1,0},{2,3},{3,2},{4,5},{5,4},{6,7},{7,6},{8,9},{9,8},{10,11... | collective-permute-start | bytes 3145736 | tf_op jit(solution)/shard_map/ppermute | solution.py:133
  17.8 0.0 copy-done.3
  17.8 2.6 %all-gather = s32[2,1,8,4]{2,3,1,0:T(4,128)S(1)} all-gather(s32[1,1,8,4]{2,3,1,0:T(4,128)S(1)} %copy-done.3), channel_id=2, replica_groups=mesh['row'=32,'rep'=8,'feat'=2] {'feat'}, dimensions={0}, use_global_device_ids=true | all-gather | bytes 384 | tf_op jit(solution)/shard_map/all_gather | solution.py:134
  20.5 0.7 copy.13.source_ref
  21.2 0.0 collective-permute-done.peer_ref
  21.2 0.0 copy-start.2
  21.2 22.8 %all-to-all-done.panel_ref = bf16[32,128,128]{2,1,0:T(8,128)(2,1)S(1)} async-done(((bf16[32,128,128]{2,1,0:T(8,128)(2,1)}), bf16[32,128,128]{2,1,0:T(8,128)(2,1)S(1)}, u32[]{:S(2)}, u32[]{:S(2)}) %all-to-all-start) | async-done | bytes 1048608 | tf_op jit(solution)/shard_map/all_to_all | solution.py:135
  43.9 0.0 copy-start
  43.9 0.0 copy-done.2
  43.9 1.0 copy-done
  44.9 3.4 %shard_map.102 = f32[8,128,128]{2,1,0:T(8,128)} custom-call(s32[8]{0:T(128)} %bitcast.12, s32[2,8,4]{2,1,0:T(8,128)} %copy.13.source_ref, bf16[8,4,128,128]{3,2,1,0:T(8,128)(2,1)} %bitcast.7, bf16[8,4,128,128]{3,2,1,0:T(8,128)(2,1)} %copy-done.2, bf16[32,128,128]{2,1,0:T(8,128)(2,1)} %copy-done), custom_call_target="tpu_custom_call" | custom-call | tf_op jit(solution)/shard_map/pallas_call | solution.py:136
  48.3 21.6 %all_to_all.25.parts_ref = f32[8,128,128]{2,1,0:T(8,128)} all-to-all(f32[8,128,128]{2,1,0:T(8,128)} %shard_map.102), channel_id=1, replica_groups=mesh['row'=32,'rep'=8,'feat'=2] {'rep'}, dimensions={0} | all-to-all | bytes 1048576 | tf_op jit(solution)/shard_map/all_to_all | solution.py:142
  69.8 1.7 %shard_map.103 = f32[256,128]{1,0:T(8,128)} custom-call(f32[8,128,128]{2,1,0:T(8,128)} %all_to_all.25.parts_ref, f32[128,128]{1,0:T(8,128)} %cotangent_ref.1), custom_call_target="tpu_custom_call" | custom-call | tf_op jit(solution)/shard_map/pallas_call | solution.py:143
  71.6 3.5 %all_gather.7.both_ref = f32[512,128]{1,0:T(8,128)} all-gather(f32[256,128]{1,0:T(8,128)} %shard_map.103), channel_id=1, replica_groups=mesh['row'=32,'rep'=8,'feat'=2] {'feat'}, dimensions={0}, use_global_device_ids=true | all-gather | bytes 393216 | tf_op jit(solution)/shard_map/all_gather | solution.py:146
  75.1 2.5 %shard_map.104 = (f32[128,128]{1,0:T(8,128)}, bf16[8,208,128]{2,1,0:T(8,128)(2,1)}) custom-call(f32[512,128]{1,0:T(8,128)} %all_gather.7.both_ref, f32[256,256]{1,0:T(8,128)} %weight_ref.1, f32[1,256]{1,0:T(1,128)} %bitcast.14), custom_call_target="tpu_custom_call" | custom-call | tf_op jit(solution)/shard_map/pallas_call | solution.py:147
  77.6 20.3 %all_to_all.26.pay_ref = bf16[8,208,128]{2,1,0:T(8,128)(2,1)} all-to-all(bf16[8,208,128]{2,1,0:T(8,128)(2,1)} %get-tuple-element.9), channel_id=1, replica_groups=mesh['row'=32,'rep'=8,'feat'=2] {'rep'}, dimensions={0} | all-to-all | bytes 851968 | tf_op jit(solution)/shard_map/all_to_all | solution.py:153
  97.8 4.4 %shard_map.105 = bf16[32,168,128]{2,1,0:T(8,128)(2,1)} custom-call(s32[8]{0:T(128)} %bitcast.13, s32[2,8,4]{2,1,0:T(8,128)} %copy.13.source_ref, bf16[8,4,128,128]{3,2,1,0:T(8,128)(2,1)} %bitcast.8, bf16[8,4,128,128]{3,2,1,0:T(8,128)(2,1)} %copy-done.2, bf16[8,208,128]{2,1,0:T(8,128)(2,1)} %all_to_all.26.pay_ref), custom_call_target="tpu_custom_call" | custom-call | tf_op jit(solution)/shard_map/pallas_call | solution.py:154
  102.2 42.2 %all_to_all.27.parts_ref = bf16[32,168,128]{2,1,0:T(8,128)(2,1)} all-to-all(bf16[32,168,128]{2,1,0:T(8,128)(2,1)} %shard_map.105), channel_id=1, replica_groups=mesh['row'=32,'rep'=8,'feat'=2] {'row'}, dimensions={0} | all-to-all | bytes 2752512 | tf_op jit(solution)/shard_map/all_to_all | solution.py:164
  144.4 2.2 %shard_map.106 = (f32[128,128]{1,0:T(8,128)}, f32[8,40,128]{2,1,0:T(8,128)}) custom-call(bf16[32,168,128]{2,1,0:T(8,128)(2,1)} %all_to_all.27.parts_ref), custom_call_target="tpu_custom_call" | custom-call | tf_op jit(solution)/shard_map/pallas_call | solution.py:165
  146.7 14.2 %all_to_all.28 = f32[8,40,128]{2,1,0:T(8,128)S(1)} all-to-all(f32[8,40,128]{2,1,0:T(8,128)} %get-tuple-element.11), channel_id=1, replica_groups=mesh['row'=32,'rep'=8,'feat'=2] {'rep'}, dimensions={0} | all-to-all | bytes 327680 | tf_op jit(solution)/shard_map/all_to_all | solution.py:171
  160.8 0.5 slice_bitcast_fusion
  161.4 0.7 slice.8
Async XLA Ops:
  0.6 15.2 %copy-start.1 = (bf16[1,1,8,4,128,128]{5,4,3,2,1,0:T(8,128)(2,1)S(1)}, bf16[1,1,8,4,128,128]{5,4,3,2,1,0:T(8,128)(2,1)}, u32[]{:S(2)}) copy-start(bf16[1,1,8,4,128,128]{5,4,3,2,1,0:T(8,128)(2,1)} %param.11) | copy-start | bytes 3145732
  0.6 17.2 %copy-start.3 = (s32[1,1,8,4]{2,3,1,0:T(4,128)S(1)}, s32[1,1,8,4]{2,3,1,0:T(4,128)}, u32[]{:S(2)}) copy-start(s32[1,1,8,4]{2,3,1,0:T(4,128)} %param.12) | copy-start | bytes 388
  2.7 41.2 %all-to-all-start = ((bf16[32,128,128]{2,1,0:T(8,128)(2,1)}), bf16[32,128,128]{2,1,0:T(8,128)(2,1)S(1)}, u32[]{:S(2)}, u32[]{:S(2)}) async-start(bf16[32,128,128]{2,1,0:T(8,128)(2,1)} %broadcast_in_dim.4), calls=%async_computation | async-start | bytes 2097152 | tf_op jit(solution)/shard_map/all_to_all | solution.py:135
  15.9 5.3 %collective-permute-start = (bf16[8,4,128,128]{3,2,1,0:T(8,128)(2,1)S(1)}, bf16[8,4,128,128]{3,2,1,0:T(8,128)(2,1)S(1)}, u32[]{:S(2)}, u32[]{:S(2)}) collective-permute-start(bf16[8,4,128,128]{3,2,1,0:T(8,128)(2,1)S(1)} %bitcast.9), channel_id=1, source_target_pairs={{0,1},{1,0},{2,3},{3,2},{4,5},{5,4},{6,7},{7,6},{8,9},{9,8},{10,11... | collective-permute-start | bytes 3145736 | tf_op jit(solution)/shard_map/ppermute | solution.py:133
  21.2 22.8 %copy-start.2 = (bf16[8,4,128,128]{3,2,1,0:T(8,128)(2,1)}, bf16[8,4,128,128]{3,2,1,0:T(8,128)(2,1)S(1)}, u32[]{:S(2)}) copy-start(bf16[8,4,128,128]{3,2,1,0:T(8,128)(2,1)S(1)} %collective-permute-done.peer_ref) | copy-start | bytes 3145732
  43.9 1.0 copy-start

commit v2 on v1

v2 whole, which is shorter than its diff:
```python
import jax
import jax.numpy as jnp
from jax import lax
from jax.experimental import pallas as pl
from jax.experimental.pallas import tpu as pltpu
from jax.sharding import Mesh, PartitionSpec as P

BF = jnp.bfloat16
F32 = jnp.float32
HI = lax.Precision.HIGHEST
VM = pl.BlockSpec(memory_space=pltpu.VMEM)
SM = pl.BlockSpec(memory_space=pltpu.SMEM)
ROOM = pltpu.CompilerParams(vmem_limit_bytes=24 << 20)


def slot_lists(own_ref, peer_ref, feat):
    return ((own_ref, feat), (peer_ref, 1 - feat))


def forward_kernel(count_ref, source_ref, own_ref, peer_ref, panel_ref, out_ref):
    feat = lax.axis_index("feat")
    dests, half = own_ref.shape[:2]
    for d in range(dests):
        lefts, rights = [], []
        for tiles_ref, side in slot_lists(own_ref, peer_ref, feat):
            for j in range(half):
                block = panel_ref[source_ref[side, d, j]]
                live = side * half + j < count_ref[d]
                lefts.append(tiles_ref[d, j])
                rights.append(jnp.where(live, block, jnp.zeros_like(block)))
        out_ref[d] = jnp.dot(
            jnp.concatenate(lefts, axis=1),
            jnp.concatenate(rights, axis=0),
            preferred_element_type=F32,
        )


def collect_kernel(parts_ref, out_ref):
    total = parts_ref[0]
    for p in range(1, parts_ref.shape[0]):
        total = total + parts_ref[p]
    out_ref[...] = total


def padded(bias_term):
    upper = bias_term.astype(BF).astype(F32)
    place = lax.broadcasted_iota(jnp.int32, (8, bias_term.shape[1]), 0)
    return jnp.where(place == 0, upper, jnp.where(place == 1, bias_term - upper, 0.0))


def folded(pad):
    return pad[0:1] + pad[1:2]


def node_kernel(aggregate_ref, cotangent_ref, weight_ref, bias_ref, out_ref, pay_ref):
    first = lax.axis_index("feat") == 0
    rows, cols = out_ref.shape
    reps = pay_ref.shape[0]
    aggregate = jnp.concatenate([aggregate_ref[:rows], aggregate_ref[rows:]], axis=1)
    cotangent = jnp.concatenate([cotangent_ref[:rows], cotangent_ref[rows:]], axis=1)
    preact = jnp.dot(aggregate, weight_ref[...], precision=HI, preferred_element_type=F32) + bias_ref[...]
    sig = jax.nn.sigmoid(preact)
    output = preact * sig
    slope = cotangent * (sig * (1.0 + preact * (1.0 - sig)))
    out_ref[...] = jnp.where(first, output[:, :cols], output[:, cols:])
    slope_own = jnp.where(first, slope[:, :cols], slope[:, cols:])
    weight_rows = jnp.where(first, weight_ref[:cols], weight_ref[cols:])
    grad_t = lax.dot_general(
        weight_rows, slope, (((1,), (1,)), ((), ())), precision=HI, preferred_element_type=F32
    ).astype(BF)
    weight_term = lax.dot_general(
        aggregate, slope_own, (((0,), (0,)), ((), ())), precision=HI, preferred_element_type=F32
    )
    pad = padded(jnp.sum(slope_own, axis=0, keepdims=True)).astype(BF)
    chunk = weight_term.shape[0] // reps
    for q in range(reps):
        pay_ref[q, :rows] = grad_t
        pay_ref[q, rows : rows + chunk] = weight_term[q * chunk : (q + 1) * chunk].astype(BF)
        pay_ref[q, rows + chunk :] = pad


def backward_kernel(count_ref, source_ref, own_ref, peer_ref, pay_ref, out_ref, total_ref, terms_ref):
    feat = lax.axis_index("feat")
    dests, half, rows = own_ref.shape[:3]
    groups = total_ref.shape[0]
    x_count = out_ref.shape[0]
    z_count = groups // x_count
    extra = pay_ref.shape[1] - rows
    total_ref[...] = jnp.zeros_like(total_ref)
    for d in range(dests):
        grad_t = pay_ref[d, :rows]
        for h, (tiles_ref, side) in enumerate(slot_lists(own_ref, peer_ref, feat)):
            product = jnp.dot(
                grad_t,
                jnp.concatenate([tiles_ref[d, j] for j in range(half)], axis=1),
                preferred_element_type=F32,
            )
            for j in range(half):
                terms_ref[(d * 2 + h) * half + j] = product[:, j * rows : (j + 1) * rows]
    for d in range(dests):
        for h, (tiles_ref, side) in enumerate(slot_lists(own_ref, peer_ref, feat)):
            for j in range(half):

                @pl.when(side * half + j < count_ref[d])
                def _(d=d, h=h, j=j, side=side):
                    source = source_ref[side, d, j]
                    total_ref[source] = total_ref[source] + terms_ref[(d * 2 + h) * half + j]

    piece = jnp.zeros((extra, rows), F32)
    for q in range(pay_ref.shape[0]):
        piece = piece + pay_ref[q, rows:].astype(F32)
    term = piece[: extra - 8]
    upper = term.astype(BF)
    lower = (term - upper.astype(F32)).astype(BF)
    pad = padded(folded(piece[extra - 8 :])).astype(BF)
    base = z_count * rows
    for x in range(x_count):
        for z in range(z_count):
            out_ref[x, z * rows : (z + 1) * rows] = total_ref[z * x_count + x].astype(BF)
        out_ref[x, base : base + extra - 8] = upper
        out_ref[x, base + extra - 8 : base + 2 * extra - 16] = lower
        out_ref[x, base + 2 * extra - 16 :] = pad


def middle_kernel(parts_ref, out_ref):
    z_count, high = out_ref.shape[:2]
    rows = parts_ref.shape[2]
    base = z_count * rows
    chunk = high - rows - 8

    def summed(start, size):
        total = parts_ref[0, start : start + size].astype(F32)
        for x in range(1, parts_ref.shape[0]):
            total = total + parts_ref[x, start : start + size].astype(F32)
        return total

    term = (summed(base, chunk) + summed(base + chunk, chunk)).astype(BF)
    pad = padded(folded(summed(base + 2 * chunk, 8))).astype(BF)
    for z in range(z_count):
        out_ref[z, :rows] = summed(z * rows, rows).astype(BF)
        out_ref[z, rows : rows + chunk] = term
        out_ref[z, rows + chunk :] = pad


def finish_kernel(parts_ref, grad_ref, bias_ref, piece_ref):
    rows = grad_ref.shape[0]
    chunk = piece_ref.shape[1]
    total = parts_ref[0].astype(F32)
    for s in range(1, parts_ref.shape[0]):
        total = total + parts_ref[s].astype(F32)
    grad_ref[...] = total[:rows].T
    bias_ref[...] = folded(total[rows + chunk :])
    for q in range(piece_ref.shape[0]):
        piece_ref[q] = total[rows : rows + chunk]


def shape(dims, dtype):
    return jax.ShapeDtypeStruct(dims, dtype)


def near(dims, dtype):
    return pltpu.VMEM(dims, dtype)


def held(array):
    return pltpu.with_memory_space_constraint(array, pltpu.VMEM)


def swap(array, axis):
    return held(lax.all_to_all(array, axis, 0, 0, tiled=True))


def local(features, weight, layer_bias, cotangent, adj_tiles, tile_source, tile_count):
    rows, cols = features.shape
    z_count, x_count = lax.axis_size("z"), lax.axis_size("x")
    n_row = z_count * x_count
    counts = tile_count[0, 0]
    dests, half = adj_tiles.shape[2:4]
    reps = lax.axis_size("rep")
    width = weight.shape[0]
    chunk = width // reps
    peer = held(lax.ppermute(adj_tiles[0, 0], "feat", [(0, 1), (1, 0)]))
    own = held(adj_tiles[0, 0])
    sources = lax.all_gather(tile_source[0, 0], "feat")
    cotangents = held(lax.all_gather(cotangent, "feat", axis=0, tiled=True))
    panel = swap(jnp.broadcast_to(features[None], (n_row, rows, cols)), ("z", "x"))
    partial = pl.pallas_call(
        forward_kernel,
        out_shape=near((dests, rows, cols), F32),
        in_specs=[SM, SM, VM, VM, VM],
        out_specs=VM,
        compiler_params=ROOM,
    )(counts, sources, own, peer, panel)
    own_aggregate = pl.pallas_call(
        collect_kernel,
        out_shape=near((rows, cols), F32),
        in_specs=[VM],
        out_specs=VM,
        compiler_params=ROOM,
    )(swap(partial, "rep"))
    aggregate = held(lax.all_gather(own_aggregate, "feat", axis=0, tiled=True))
    output, pay = pl.pallas_call(
        node_kernel,
        out_shape=(shape((rows, cols), F32), near((reps, rows + chunk + 8, cols), BF)),
        in_specs=[VM, VM, VM, VM],
        out_specs=(VM, VM),
        compiler_params=ROOM,
    )(aggregate, cotangents, held(weight), layer_bias[None])
    sends = pl.pallas_call(
        backward_kernel,
        out_shape=near((x_count, z_count * rows + 2 * chunk + 8, cols), BF),
        in_specs=[SM, SM, VM, VM, VM],
        out_specs=VM,
        compiler_params=ROOM,
        scratch_shapes=[
            pltpu.VMEM((n_row, cols, rows), F32),
            pltpu.VMEM((dests * 2 * half, cols, rows), F32),
        ],
    )(counts, sources, own, peer, swap(pay, "rep"))
    onward = pl.pallas_call(
        middle_kernel,
        out_shape=near((z_count, rows + chunk + 8, cols), BF),
        in_specs=[VM],
        out_specs=VM,
        compiler_params=ROOM,
    )(swap(sends, "x"))
    grad_features, grad_bias, pieces = pl.pallas_call(
        finish_kernel,
        out_shape=(shape((rows, cols), F32), shape((1, cols), F32), near((reps, chunk, cols), F32)),
        in_specs=[VM],
        out_specs=(VM, VM, VM),
        compiler_params=ROOM,
    )(swap(onward, "z"))
    grad_weight = lax.all_to_all(pieces, "rep", 0, 0, tiled=True).reshape(width, cols)
    return output, grad_features, grad_weight, grad_bias[0]


def solution(mesh):
    n_row, n_rep, n_feat = mesh.devices.shape
    x_count = 4 if n_row > 4 else 2
    fine = Mesh(mesh.devices.reshape(n_row // x_count, x_count, n_rep, n_feat), ("z", "x", "rep", "feat"))
    nodes = P(("z", "x", "rep"), "feat")
    in_specs = (
        nodes,
        P(),
        P(),
        nodes,
        P(("z", "x"), "rep", None, "feat", None, None),
        P(("z", "x"), "rep", None, "feat"),
        P(("z", "x"), "rep", None),
    )
    out_specs = (nodes, nodes, P(None, "feat"), P("feat"))
    return jax.shard_map(local, mesh=fine, in_specs=in_specs, out_specs=out_specs, check_vma=False)
```

time: 163 us -> 140 us (0.86)
  the two profiles are of different devices: /device:TPU:8 before, /device:TPU:2 now
where the time goes in v2:
time: 140 us; the launch traced here: 139 us
  blocking collectives  69.3 us (50%)
  waiting for transfers between devices  37.1 us (26%)
  starting transfers between devices  22.7 us (16%)
  Pallas kernels  5.66 us (4%)
  local copies, waits for them, and re-layouts  3.52 us (3%)
    all_to_all x3, blocking collectives, swap(): return held(lax.all_to_all(array, axis, 0, 0, tiled=True))  51.4 us
    all_to_all x2, waiting for transfers between devices, swap(): return held(lax.all_to_all(array, axis, 0, 0, tiled=True))  37.1 us
    all_to_all x2, starting transfers between devices, swap(): return held(lax.all_to_all(array, axis, 0, 0, tiled=True))  20.8 us
    all_to_all x1, blocking collectives, local(): lax.all_to_all(pieces, 'rep', 0, 0, tiled=True).reshape(width, cols)  11.5 us
  transfers between devices with their start and end apart: 3, of which 2 were waited for; matrix products, arithmetic and copies ran while one was open for 0% of the time, Pallas kernels for 0%

profile of v2, /device:TPU:2, one launch (start us, length us, event | category | flops | bytes accessed | tf_op | source)
XLA Modules:
  0.0 139.1 jit_solution(1245615436632443668)
XLA Ops:
  0.6 2.0 %broadcast_in_dim.4 = bf16[32,128,128]{2,1,0:T(8,128)(2,1)} broadcast(bf16[128,128]{1,0:T(8,128)(2,1)} %param.7), dimensions={1,2} | broadcast | bytes 1081344 | tf_op jit(solution)/shard_map/broadcast_in_dim | solution.py:186
  2.6 0.0 copy-start
  2.6 0.0 copy-start.6
  2.6 0.0 copy-start.3
  2.6 13.6 %all-to-all-start = ((bf16[32,128,128]{2,1,0:T(8,128)(2,1)}), bf16[32,128,128]{2,1,0:T(8,128)(2,1)S(1)}, u32[]{:S(2)}, u32[]{:S(2)}) async-start(bf16[32,128,128]{2,1,0:T(8,128)(2,1)} %broadcast_in_dim.4), calls=%async_computation | async-start | bytes 2097152 | tf_op jit(solution)/shard_map/all_to_all | solution.py:170
  16.2 0.0 copy-done
  16.2 1.9 %collective-permute-start = (bf16[8,4,128,128]{3,2,1,0:T(8,128)(2,1)S(1)}, bf16[8,4,128,128]{3,2,1,0:T(8,128)(2,1)S(1)}, u32[]{:S(2)}, u32[]{:S(2)}) collective-permute-start(bf16[8,4,128,128]{3,2,1,0:T(8,128)(2,1)S(1)} %bitcast.6), channel_id=1, source_target_pairs={{0,1},{1,0},{2,3},{3,2},{4,5},{5,4},{6,7},{7,6},{8,9},{9,8},{10,11... | collective-permute-start | bytes 3145736 | tf_op jit(solution)/shard_map/ppermute | solution.py:182
  18.1 0.0 copy-done.6
  18.2 2.6 %all-gather = s32[2,1,8,4]{2,3,1,0:T(4,128)S(1)} all-gather(s32[1,1,8,4]{2,3,1,0:T(4,128)S(1)} %copy-done.6), channel_id=2, replica_groups=mesh['z'=8,'x'=4,'rep'=8,'feat'=2] {'feat'}, dimensions={0}, use_global_device_ids=true | all-gather | bytes 384 | tf_op jit(solution)/shard_map/all_gather | solution.py:184
  20.8 0.1 copy.13.source_ref
  20.9 0.0 collective-permute-done.peer_ref
  20.9 23.4 %all-to-all-done.panel_ref = bf16[32,128,128]{2,1,0:T(8,128)(2,1)S(1)} async-done(((bf16[32,128,128]{2,1,0:T(8,128)(2,1)}), bf16[32,128,128]{2,1,0:T(8,128)(2,1)S(1)}, u32[]{:S(2)}, u32[]{:S(2)}) %all-to-all-start) | async-done | bytes 1048608 | tf_op jit(solution)/shard_map/all_to_all | solution.py:170
  44.3 0.0 copy-done.3
  44.3 1.4 %shard_map.102 = f32[8,128,128]{2,1,0:T(8,128)S(1)} custom-call(s32[8]{0:T(128)S(1)} %bitcast.9, s32[2,8,4]{2,1,0:T(8,128)S(1)} %copy.13.source_ref, bf16[8,4,128,128]{3,2,1,0:T(8,128)(2,1)S(1)} %bitcast.7, bf16[8,4,128,128]{3,2,1,0:T(8,128)(2,1)S(1)} %collective-permute-done.peer_ref, bf16[32,128,128]{2,1,0:T(8,128)(2,1)S(1)} %all-to-all-done.panel_ref), custom_call_target="tpu_custom_call" | custom-call | tf_op jit(solution)/shard_map/pallas_call | solution.py:187
  45.7 0.0 copy-start.1
  45.7 0.8 copy-done.1
  46.5 7.2 %all-to-all-start.1 = ((f32[8,128,128]{2,1,0:T(8,128)}), f32[8,128,128]{2,1,0:T(8,128)S(1)}, u32[]{:S(2)}, u32[]{:S(2)}) async-start(f32[8,128,128]{2,1,0:T(8,128)} %copy-done.1), calls=%async_computation.1 | async-start | bytes 1048576 | tf_op jit(solution)/shard_map/all_to_all | solution.py:170
  53.7 0.0 copy-done.5
  53.7 1.9 %all_gather.11.cotangent_ref = f32[256,128]{1,0:T(8,128)S(1)} all-gather(f32[128,128]{1,0:T(8,128)S(1)} %copy-done.5), channel_id=1, replica_groups=mesh['z'=8,'x'=4,'rep'=8,'feat'=2] {'feat'}, dimensions={0}, use_global_device_ids=true | all-gather | bytes 196608 | tf_op jit(solution)/shard_map/all_gather | solution.py:185
  55.6 13.8 %all-to-all-done.1.parts_ref = f32[8,128,128]{2,1,0:T(8,128)S(1)} async-done(((f32[8,128,128]{2,1,0:T(8,128)}), f32[8,128,128]{2,1,0:T(8,128)S(1)}, u32[]{:S(2)}, u32[]{:S(2)}) %all-to-all-start.1) | async-done | bytes 524320 | tf_op jit(solution)/shard_map/all_to_all | solution.py:170
  69.4 1.9 %all_gather.10.aggregate_ref = f32[256,128]{1,0:T(8,128)S(1)} all-gather(f32[128,128]{1,0:T(8,128)S(1)} %shard_map.103), channel_id=1, replica_groups=mesh['z'=8,'x'=4,'rep'=8,'feat'=2] {'feat'}, dimensions={0}, use_global_device_ids=true | all-gather | bytes 196608 | tf_op jit(solution)/shard_map/all_gather | solution.py:201
  71.3 0.0 copy-done.2
  71.3 0.0 copy-done.4
  71.3 1.0 shard_map.104
  72.3 16.6 %all_to_all.30.pay_ref = bf16[8,168,128]{2,1,0:T(8,128)(2,1)S(1)} all-to-all(bf16[8,168,128]{2,1,0:T(8,128)(2,1)S(1)} %get-tuple-element.10), channel_id=1, replica_groups=mesh['z'=8,'x'=4,'rep'=8,'feat'=2] {'rep'}, dimensions={0} | all-to-all | bytes 688128 | tf_op jit(solution)/shard_map/all_to_all | solution.py:170
  88.9 2.3 %shard_map.105 = bf16[4,1096,128]{2,1,0:T(8,128)(2,1)S(1)} custom-call(s32[8]{0:T(128)S(1)} %bitcast.10, s32[2,8,4]{2,1,0:T(8,128)S(1)} %copy.13.source_ref, bf16[8,4,128,128]{3,2,1,0:T(8,128)(2,1)S(1)} %bitcast.8, bf16[8,4,128,128]{3,2,1,0:T(8,128)(2,1)S(1)} %collective-permute-done.peer_ref, bf16[8,168,128]{2,1,0:T(8,128)(2,1)S(1)} %all_to_all.30.pay_ref), custom_call_target="tpu_custom_call" | custom-call | tf_op jit(solution)/shard_map/pallas_call | solution.py:209
  91.3 19.5 %all_to_all.31.parts_ref = bf16[4,1096,128]{2,1,0:T(8,128)(2,1)S(1)} all-to-all(bf16[4,1096,128]{2,1,0:T(8,128)(2,1)S(1)} %shard_map.105), channel_id=1, replica_groups=mesh['z'=8,'x'=4,'rep'=8,'feat'=2] {'x'}, dimensions={0} | all-to-all | bytes 2244608 | tf_op jit(solution)/shard_map/all_to_all | solution.py:170
  110.8 0.1 shard_map.106
  110.9 15.3 %all_to_all.32.parts_ref = bf16[8,168,128]{2,1,0:T(8,128)(2,1)S(1)} all-to-all(bf16[8,168,128]{2,1,0:T(8,128)(2,1)S(1)} %shard_map.106), channel_id=1, replica_groups=mesh['z'=8,'x'=4,'rep'=8,'feat'=2] {'z'}, dimensions={0} | all-to-all | bytes 688128 | tf_op jit(solution)/shard_map/all_to_all | solution.py:170
  126.3 0.7 shard_map.107
  127.0 11.5 %all_to_all.33 = f32[8,32,128]{2,1,0:T(8,128)S(1)} all-to-all(f32[8,32,128]{2,1,0:T(8,128)S(1)} %get-tuple-element.12), channel_id=1, replica_groups=mesh['z'=8,'x'=4,'rep'=8,'feat'=2] {'rep'}, dimensions={0} | all-to-all | bytes 262144 | tf_op jit(solution)/shard_map/all_to_all | solution.py:234
  138.5 0.7 copy.16
  (4 shorter events, 0.0 us)
Async XLA Ops:
  2.6 13.6 %copy-start = (bf16[1,1,8,4,128,128]{5,4,3,2,1,0:T(8,128)(2,1)S(1)}, bf16[1,1,8,4,128,128]{5,4,3,2,1,0:T(8,128)(2,1)}, u32[]{:S(2)}) copy-start(bf16[1,1,8,4,128,128]{5,4,3,2,1,0:T(8,128)(2,1)} %param.11) | copy-start | bytes 3145732
  2.6 15.5 %copy-start.6 = (s32[1,1,8,4]{2,3,1,0:T(4,128)S(1)}, s32[1,1,8,4]{2,3,1,0:T(4,128)}, u32[]{:S(2)}) copy-start(s32[1,1,8,4]{2,3,1,0:T(4,128)} %param.12) | copy-start | bytes 388
  2.6 41.7 %copy-start.3 = (s32[1,1,8]{2,1,0:T(1,128)S(1)}, s32[1,1,8]{2,1,0:T(1,128)}, u32[]{:S(2)}) copy-start(s32[1,1,8]{2,1,0:T(1,128)} %param.13) | copy-start | bytes 100
  2.6 41.7 %all-to-all-start = ((bf16[32,128,128]{2,1,0:T(8,128)(2,1)}), bf16[32,128,128]{2,1,0:T(8,128)(2,1)S(1)}, u32[]{:S(2)}, u32[]{:S(2)}) async-start(bf16[32,128,128]{2,1,0:T(8,128)(2,1)} %broadcast_in_dim.4), calls=%async_computation | async-start | bytes 2097152 | tf_op jit(solution)/shard_map/all_to_all | solution.py:170
  16.2 4.7 %collective-permute-start = (bf16[8,4,128,128]{3,2,1,0:T(8,128)(2,1)S(1)}, bf16[8,4,128,128]{3,2,1,0:T(8,128)(2,1)S(1)}, u32[]{:S(2)}, u32[]{:S(2)}) collective-permute-start(bf16[8,4,128,128]{3,2,1,0:T(8,128)(2,1)S(1)} %bitcast.6), channel_id=1, source_target_pairs={{0,1},{1,0},{2,3},{3,2},{4,5},{5,4},{6,7},{7,6},{8,9},{9,8},{10,11... | collective-permute-start | bytes 3145736 | tf_op jit(solution)/shard_map/ppermute | solution.py:182
  44.3 9.4 %copy-start.5 = (f32[128,128]{1,0:T(8,128)S(1)}, f32[128,128]{1,0:T(8,128)}, u32[]{:S(2)}) copy-start(f32[128,128]{1,0:T(8,128)} %param.10) | copy-start | bytes 196612
  45.7 0.8 copy-start.1
  46.5 24.8 %copy-start.2 = (f32[256,256]{1,0:T(8,128)S(1)}, f32[256,256]{1,0:T(8,128)}, u32[]{:S(2)}) copy-start(f32[256,256]{1,0:T(8,128)} %weight_ref.1) | copy-start | bytes 786436
  46.5 24.8 %copy-start.4 = (f32[256]{0:T(256)S(1)}, f32[256]{0:T(256)}, u32[]{:S(2)}) copy-start(f32[256]{0:T(256)} %param.9) | copy-start | bytes 3076
  46.5 22.9 %all-to-all-start.1 = ((f32[8,128,128]{2,1,0:T(8,128)}), f32[8,128,128]{2,1,0:T(8,128)S(1)}, u32[]{:S(2)}, u32[]{:S(2)}) async-start(f32[8,128,128]{2,1,0:T(8,128)} %copy-done.1), calls=%async_computation.1 | async-start | bytes 1048576 | tf_op jit(solution)/shard_map/all_to_all | solution.py:170

commit v3 on v2

--- a/solution.py
+++ b/solution.py
@@ -184,6 +184,9 @@
     sources = lax.all_gather(tile_source[0, 0], "feat")
     cotangents = held(lax.all_gather(cotangent, "feat", axis=0, tiled=True))
     panel = swap(jnp.broadcast_to(features[None], (n_row, rows, cols)), ("z", "x"))
+    panel, cotangents, near_weight, near_bias = lax.optimization_barrier(
+        (panel, cotangents, held(weight), held(layer_bias[None]))
+    )
     partial = pl.pallas_call(
         forward_kernel,
         out_shape=near((dests, rows, cols), F32),
@@ -205,7 +208,7 @@
         in_specs=[VM, VM, VM, VM],
         out_specs=(VM, VM),
         compiler_params=ROOM,
-    )(aggregate, cotangents, held(weight), layer_bias[None])
+    )(aggregate, cotangents, near_weight, near_bias)
     sends = pl.pallas_call(
         backward_kernel,
         out_shape=near((x_count, z_count * rows + 2 * chunk + 8, cols), BF),

time: 140 us -> 139 us (level)
  blocking collectives: 69.3 us -> 92.1 us
  waiting for transfers between devices: 37.1 us -> 21.5 us
  starting transfers between devices: 22.7 us -> 15.5 us
    all_to_all x3 -> x4, blocking collectives: 51.4 us -> 74.2 us  [swap(): return held(lax.all_to_all(array, axis, 0, 0, tiled=True))]
    all_to_all x2 -> x1, waiting for transfers between devices: 37.1 us -> 21.5 us  [swap(): return held(lax.all_to_all(array, axis, 0, 0, tiled=True))]
    all_to_all x2 -> x1, starting transfers between devices: 20.8 us -> 13.6 us  [swap(): return held(lax.all_to_all(array, axis, 0, 0, tiled=True))]
  transfers between devices with their start and end apart: 3 -> 2, of which waited for: 2 -> 1; matrix products, arithmetic and copies ran while one was open for 0% -> 0% of each run, Pallas kernels for 0% -> 0%
where the time goes in v3:
time: 139 us; the launch traced here: 138 us
  blocking collectives  92.1 us (66%)
  waiting for transfers between devices  21.5 us (15%)
  starting transfers between devices  15.5 us (11%)
  Pallas kernels  5.66 us (4%)
  local copies, waits for them, and re-layouts  2.74 us (2%)
    all_to_all x4, blocking collectives, swap(): return held(lax.all_to_all(array, axis, 0, 0, tiled=True))  74.2 us
    all_to_all x1, waiting for transfers between devices, swap(): return held(lax.all_to_all(array, axis, 0, 0, tiled=True))  21.5 us
    all_to_all x1, starting transfers between devices, swap(): return held(lax.all_to_all(array, axis, 0, 0, tiled=True))  13.6 us
    all_to_all x1, blocking collectives, local(): lax.all_to_all(pieces, 'rep', 0, 0, tiled=True).reshape(width, cols)  11.5 us
  transfers between devices with their start and end apart: 2, of which 1 were waited for; matrix products, arithmetic and copies ran while one was open for 0% of the time, Pallas kernels for 0%

profile of v3, /device:TPU:2, one launch (start us, length us, event | category | flops | bytes accessed | tf_op | source)
XLA Modules:
  0.0 138.2 jit_solution(10205507984017960418)
XLA Ops:
  0.6 2.0 %broadcast_in_dim.4 = bf16[32,128,128]{2,1,0:T(8,128)(2,1)} broadcast(bf16[128,128]{1,0:T(8,128)(2,1)} %param.7), dimensions={1,2} | broadcast | bytes 1081344 | tf_op jit(solution)/shard_map/broadcast_in_dim | solution.py:186
  2.6 0.0 copy-start
  2.6 0.0 copy-start.5
  2.6 0.0 copy-start.4
  2.6 0.0 copy-start.2
  2.6 13.6 %all-to-all-start = ((bf16[32,128,128]{2,1,0:T(8,128)(2,1)}), bf16[32,128,128]{2,1,0:T(8,128)(2,1)S(1)}, u32[]{:S(2)}, u32[]{:S(2)}) async-start(bf16[32,128,128]{2,1,0:T(8,128)(2,1)} %broadcast_in_dim.4), calls=%async_computation | async-start | bytes 2097152 | tf_op jit(solution)/shard_map/all_to_all | solution.py:170
  16.2 0.0 copy-done
  16.2 1.9 %collective-permute-start = (bf16[8,4,128,128]{3,2,1,0:T(8,128)(2,1)S(1)}, bf16[8,4,128,128]{3,2,1,0:T(8,128)(2,1)S(1)}, u32[]{:S(2)}, u32[]{:S(2)}) collective-permute-start(bf16[8,4,128,128]{3,2,1,0:T(8,128)(2,1)S(1)} %bitcast.6), channel_id=1, source_target_pairs={{0,1},{1,0},{2,3},{3,2},{4,5},{5,4},{6,7},{7,6},{8,9},{9,8},{10,11... | collective-permute-start | bytes 3145736 | tf_op jit(solution)/shard_map/ppermute | solution.py:182
  18.2 0.0 copy-done.5
  18.2 2.6 %all-gather = s32[2,1,8,4]{2,3,1,0:T(4,128)S(1)} all-gather(s32[1,1,8,4]{2,3,1,0:T(4,128)S(1)} %copy-done.5), channel_id=2, replica_groups=mesh['z'=8,'x'=4,'rep'=8,'feat'=2] {'feat'}, dimensions={0}, use_global_device_ids=true | all-gather | bytes 384 | tf_op jit(solution)/shard_map/all_gather | solution.py:184
  20.8 0.1 copy.13.source_ref
  20.9 0.0 copy-done.4
  20.9 1.9 %all_gather.10.cotangent_ref = f32[256,128]{1,0:T(8,128)S(1)} all-gather(f32[128,128]{1,0:T(8,128)S(1)} %copy-done.4), channel_id=1, replica_groups=mesh['z'=8,'x'=4,'rep'=8,'feat'=2] {'feat'}, dimensions={0}, use_global_device_ids=true | all-gather | bytes 196608 | tf_op jit(solution)/shard_map/all_gather | solution.py:185
  22.8 21.5 %all-to-all-done.panel_ref = bf16[32,128,128]{2,1,0:T(8,128)(2,1)S(1)} async-done(((bf16[32,128,128]{2,1,0:T(8,128)(2,1)}), bf16[32,128,128]{2,1,0:T(8,128)(2,1)S(1)}, u32[]{:S(2)}, u32[]{:S(2)}) %all-to-all-start) | async-done | bytes 1048608 | tf_op jit(solution)/shard_map/all_to_all | solution.py:170
  44.3 0.0 collective-permute-done.peer_ref
  44.3 0.0 copy-done.2
  44.3 1.4 %shard_map.102 = f32[8,128,128]{2,1,0:T(8,128)S(1)} custom-call(s32[8]{0:T(128)S(1)} %bitcast.9, s32[2,8,4]{2,1,0:T(8,128)S(1)} %copy.13.source_ref, bf16[8,4,128,128]{3,2,1,0:T(8,128)(2,1)S(1)} %bitcast.7, bf16[8,4,128,128]{3,2,1,0:T(8,128)(2,1)S(1)} %collective-permute-done.peer_ref, bf16[32,128,128]{2,1,0:T(8,128)(2,1)S(1)} %all-to-all-done.panel_ref), custom_call_target="tpu_custom_call" | custom-call | tf_op jit(solution)/shard_map/pallas_call | solution.py:190
  45.7 0.0 copy-start.1
  45.7 0.0 copy-start.3
  45.7 22.7 %all_to_all.30.parts_ref = f32[8,128,128]{2,1,0:T(8,128)S(1)} all-to-all(f32[8,128,128]{2,1,0:T(8,128)S(1)} %shard_map.102), channel_id=1, replica_groups=mesh['z'=8,'x'=4,'rep'=8,'feat'=2] {'rep'}, dimensions={0} | all-to-all | bytes 1048576 | tf_op jit(solution)/shard_map/all_to_all | solution.py:170
  68.4 1.9 %all_gather.11.aggregate_ref = f32[256,128]{1,0:T(8,128)S(1)} all-gather(f32[128,128]{1,0:T(8,128)S(1)} %shard_map.103), channel_id=1, replica_groups=mesh['z'=8,'x'=4,'rep'=8,'feat'=2] {'feat'}, dimensions={0}, use_global_device_ids=true | all-gather | bytes 196608 | tf_op jit(solution)/shard_map/all_gather | solution.py:204
  70.3 0.0 copy-done.1
  70.3 0.0 copy-done.3
  70.4 1.0 shard_map.104
  71.4 16.6 %all_to_all.31.pay_ref = bf16[8,168,128]{2,1,0:T(8,128)(2,1)S(1)} all-to-all(bf16[8,168,128]{2,1,0:T(8,128)(2,1)S(1)} %get-tuple-element.18), channel_id=1, replica_groups=mesh['z'=8,'x'=4,'rep'=8,'feat'=2] {'rep'}, dimensions={0} | all-to-all | bytes 688128 | tf_op jit(solution)/shard_map/all_to_all | solution.py:170
  88.0 2.3 %shard_map.105 = bf16[4,1096,128]{2,1,0:T(8,128)(2,1)S(1)} custom-call(s32[8]{0:T(128)S(1)} %bitcast.10, s32[2,8,4]{2,1,0:T(8,128)S(1)} %copy.13.source_ref, bf16[8,4,128,128]{3,2,1,0:T(8,128)(2,1)S(1)} %bitcast.8, bf16[8,4,128,128]{3,2,1,0:T(8,128)(2,1)S(1)} %collective-permute-done.peer_ref, bf16[8,168,128]{2,1,0:T(8,128)(2,1)S(1)} %all_to_all.31.pay_ref), custom_call_target="tpu_custom_call" | custom-call | tf_op jit(solution)/shard_map/pallas_call | solution.py:212
  90.3 19.6 %all_to_all.32.parts_ref = bf16[4,1096,128]{2,1,0:T(8,128)(2,1)S(1)} all-to-all(bf16[4,1096,128]{2,1,0:T(8,128)(2,1)S(1)} %shard_map.105), channel_id=1, replica_groups=mesh['z'=8,'x'=4,'rep'=8,'feat'=2] {'x'}, dimensions={0} | all-to-all | bytes 2244608 | tf_op jit(solution)/shard_map/all_to_all | solution.py:170
  109.9 0.1 shard_map.106
  110.0 15.3 %all_to_all.33.parts_ref = bf16[8,168,128]{2,1,0:T(8,128)(2,1)S(1)} all-to-all(bf16[8,168,128]{2,1,0:T(8,128)(2,1)S(1)} %shard_map.106), channel_id=1, replica_groups=mesh['z'=8,'x'=4,'rep'=8,'feat'=2] {'z'}, dimensions={0} | all-to-all | bytes 688128 | tf_op jit(solution)/shard_map/all_to_all | solution.py:170
  125.4 0.7 shard_map.107
  126.1 11.5 %all_to_all.34 = f32[8,32,128]{2,1,0:T(8,128)S(1)} all-to-all(f32[8,32,128]{2,1,0:T(8,128)S(1)} %get-tuple-element.20), channel_id=1, replica_groups=mesh['z'=8,'x'=4,'rep'=8,'feat'=2] {'rep'}, dimensions={0} | all-to-all | bytes 262144 | tf_op jit(solution)/shard_map/all_to_all | solution.py:237
  137.6 0.7 copy.16
  (1 shorter events, 0.0 us)
Async XLA Ops:
  2.6 13.6 %copy-start = (bf16[1,1,8,4,128,128]{5,4,3,2,1,0:T(8,128)(2,1)S(1)}, bf16[1,1,8,4,128,128]{5,4,3,2,1,0:T(8,128)(2,1)}, u32[]{:S(2)}) copy-start(bf16[1,1,8,4,128,128]{5,4,3,2,1,0:T(8,128)(2,1)} %param.11) | copy-start | bytes 3145732
  2.6 15.6 %copy-start.5 = (s32[1,1,8,4]{2,3,1,0:T(4,128)S(1)}, s32[1,1,8,4]{2,3,1,0:T(4,128)}, u32[]{:S(2)}) copy-start(s32[1,1,8,4]{2,3,1,0:T(4,128)} %param.12) | copy-start | bytes 388
  2.6 18.3 %copy-start.4 = (f32[128,128]{1,0:T(8,128)S(1)}, f32[128,128]{1,0:T(8,128)}, u32[]{:S(2)}) copy-start(f32[128,128]{1,0:T(8,128)} %param.10) | copy-start | bytes 196612
  2.6 41.7 %copy-start.2 = (s32[1,1,8]{2,1,0:T(1,128)S(1)}, s32[1,1,8]{2,1,0:T(1,128)}, u32[]{:S(2)}) copy-start(s32[1,1,8]{2,1,0:T(1,128)} %param.13) | copy-start | bytes 100
  2.6 41.7 %all-to-all-start = ((bf16[32,128,128]{2,1,0:T(8,128)(2,1)}), bf16[32,128,128]{2,1,0:T(8,128)(2,1)S(1)}, u32[]{:S(2)}, u32[]{:S(2)}) async-start(bf16[32,128,128]{2,1,0:T(8,128)(2,1)} %broadcast_in_dim.4), calls=%async_computation | async-start | bytes 2097152 | tf_op jit(solution)/shard_map/all_to_all | solution.py:170
  16.2 28.1 %collective-permute-start = (bf16[8,4,128,128]{3,2,1,0:T(8,128)(2,1)S(1)}, bf16[8,4,128,128]{3,2,1,0:T(8,128)(2,1)S(1)}, u32[]{:S(2)}, u32[]{:S(2)}) collective-permute-start(bf16[8,4,128,128]{3,2,1,0:T(8,128)(2,1)S(1)} %bitcast.6), channel_id=1, source_target_pairs={{0,1},{1,0},{2,3},{3,2},{4,5},{5,4},{6,7},{7,6},{8,9},{9,8},{10,11... | collective-permute-start | bytes 3145736 | tf_op jit(solution)/shard_map/ppermute | solution.py:182
  45.7 24.6 %copy-start.1 = (f32[256,256]{1,0:T(8,128)S(1)}, f32[256,256]{1,0:T(8,128)}, u32[]{:S(2)}) copy-start(f32[256,256]{1,0:T(8,128)} %weight_ref) | copy-start | bytes 786436
  45.7 24.6 %copy-start.3 = (f32[256]{0:T(256)S(1)}, f32[256]{0:T(256)}, u32[]{:S(2)}) copy-start(f32[256]{0:T(256)} %param.9) | copy-start | bytes 3076
